TPU v7x, 32 devices: a whole 2x2x4 slice. The times are simulated.
32 devices in a mesh: gx: 8 (over z, y), gy: 4 (over x, core).
Axes of the slice: x: 2, y: 2, z: 4, core: 2. Of those that a mesh axis runs over, the one named last changes fastest.
Arguments:
- right_side: float32 [64, 128, 128], P('gy', 'gx'), may hold values from -6 to 9
- diagonal: float32 [64, 128, 128], P('gy', 'gx'), may hold values from 0.02 to 0.5
- horizontal: float32 [64, 128, 128], P('gy', 'gx'), may hold values from 0.1 to 1
- vertical: float32 [128], replicated, may hold values from 0.2 to 2
- precond: float32 [2, 128, 128], replicated, may hold values from -4 to 4
- edge_rows: int32 [2, 64], replicated, may hold values from 0 to 63, as said below
Outputs:
- solution_field: float32 [64, 128, 128], P('gy', 'gx')
- residual: float32 [64, 128, 128], P('gy', 'gx')
- residual_sq: float32 [3], replicated
Inputs may be any that keep to these rules, and one draw needn't show every extreme that they name: Each row of edge_rows lists every number 0 to 63 exactly once.
All inputs are finite; a program needn't handle non-finite values.
Results may differ from a plain program's by a relative error of at most 0.00014.
Values sent between devices are 32-bit elements; how exact they have to be, the bound alone decides.
No kernel may reach another device: no remote copies, remote signals or barrier semaphores. Data moves between devices by JAX's collectives and lax.ppermute only.
A program may use at most 64 MiB of HBM per device.

v0:
```python
import jax
import jax.numpy as jnp
from jax import lax
from jax.sharding import PartitionSpec as P

ITERS = 3


def padded(x, sides, width, wrap):
    for axis, dim in sides:
        devices, length = (lax.axis_size(axis), x.shape[dim])
        up = [(i, (i + 1) % devices) for i in range(devices if wrap else devices - 1)]
        down = [(j, i) for i, j in up]
        last = lax.slice_in_dim(x, length - width, length, axis=dim)
        initial = lax.slice_in_dim(x, 0, width, axis=dim)
        before = lax.ppermute(last, axis, up)
        after = lax.ppermute(initial, axis, down)
        x = jnp.concatenate([before, x, after], axis=dim)
    return x


def local_product(left, right):
    return jnp.sum(left * right)


def on_device(right_side, diagonal, horizontal, vertical, precond, edge_rows):
    rows, cols, levels = right_side.shape
    n_gx = lax.axis_size("gx")
    n_gy = lax.axis_size("gy")
    col_index = lax.axis_index("gx")
    row_index = lax.axis_index("gy")
    total_cells = float(rows * cols * levels * n_gx * n_gy)
    half = n_gx // 2
    panel = (col_index >= half).astype(jnp.int32)
    matrix = lax.dynamic_index_in_dim(precond, panel, 0, keepdims=False)
    east_table = jnp.where(col_index == half - 1, edge_rows[0], edge_rows[1])
    west_table = jnp.where(col_index == half, edge_rows[0], edge_rows[1])
    first_row = row_index * rows
    east_local = lax.dynamic_slice_in_dim(east_table, first_row, rows)
    west_local = lax.dynamic_slice_in_dim(west_table, first_row, rows)
    east_border = (col_index == half - 1) | (col_index == n_gx - 1)
    west_border = (col_index == half) | (col_index == 0)
    solution_field = jnp.zeros_like(right_side)
    residual = right_side
    directions = []
    images = []
    norms = []
    for step in range(ITERS):
        pre = jnp.einsum("yxl,kl->yxk", residual, matrix, precision=lax.Precision.HIGHEST)
        wide = padded(pre, (("gx", 1),), 1, True)
        edges = jnp.stack([wide[:, 0], wide[:, -1]], 0)
        whole = lax.all_gather(edges, "gy", axis=1, tiled=True)
        west_fix = jnp.take(whole[0], west_local, axis=0)
        east_fix = jnp.take(whole[1], east_local, axis=0)
        west = jnp.where(west_border, west_fix, edges[0])
        east = jnp.where(east_border, east_fix, edges[1])
        tall = padded(pre, (("gy", 0),), 1, False)
        flat = jnp.pad(pre, ((0, 0), (0, 0), (1, 1)))
        east_side = jnp.concatenate([pre[:, 1:], east[:, None]], 1)
        west_side = jnp.concatenate([west[:, None], pre[:, :-1]], 1)
        beside = east_side + west_side + tall[2:] + tall[:-2]
        column = flat[:, :, 2:] + flat[:, :, :-2]
        image = diagonal * pre + horizontal * (4.0 * pre - beside) + vertical * (2.0 * pre - column)
        count = len(images)
        terms = [local_product(image, older) for older in images]
        terms = terms + [local_product(residual, older) for older in images]
        terms = terms + [local_product(image, image), local_product(residual, image)]
        if step > 0:
            terms.append(local_product(residual, residual))
        totals = lax.psum(jnp.stack(terms), ("gx", "gy")) / total_cells
        coeffs = totals[:count]
        against = totals[count : 2 * count]
        square = totals[2 * count] - jnp.sum(coeffs * coeffs)
        along = totals[2 * count + 1] - jnp.sum(coeffs * against)
        if step > 0:
            norms.append(totals[2 * count + 2])
        for number in range(count):
            pre = pre - coeffs[number] * directions[number]
            image = image - coeffs[number] * images[number]
        scale = 1.0 / jnp.sqrt(square)
        alpha = along * scale
        direction = pre * scale
        image = image * scale
        solution_field = solution_field + alpha * direction
        residual = residual - alpha * image
        directions.append(direction)
        images.append(image)
    norms.append(lax.psum(local_product(residual, residual), ("gx", "gy")) / total_cells)
    return (solution_field, residual, jnp.stack(norms))


def solution(mesh):
    in_specs = (P("gy", "gx", None), P("gy", "gx", None), P("gy", "gx", None), P(), P(), P())
    out_specs = (P("gy", "gx", None), P("gy", "gx", None), P())
    return jax.shard_map(
        on_device, mesh=mesh, in_specs=in_specs, out_specs=out_specs, check_vma=False
    )
```

profile of v0, /device:TPU:0, one launch (start us, length us, event | category | flops | bytes accessed | tf_op | source)
XLA Modules:
  0.0 243.0 jit_solution(2497374235617542815)
XLA Ops:
  0.7 0.9 copy-done
  1.5 1.2 convolution_bitcast_fusion
  2.7 1.3 collective-permute-start.2
  4.0 3.0 %collective-permute-start.3 = (f32[1,16,128]{2,1,0:T(8,128)S(1)}, f32[1,16,128]{2,1,0:T(8,128)S(1)}, u32[]{:S(2)}, u32[]{:S(2)}) collective-permute-start(f32[1,16,128]{2,1,0:T(8,128)S(1)} %get-tuple-element.48), channel_id=1, source_target_pairs={{0,1},{1,2},{2,3},{4,5},{5,6},{6,7},{8,9},{9,10},{10,11},{12,13},{... | collective-permute-start | bytes 24584 | tf_op jit(solution)/shard_map/ppermute | solution.py:16
  7.1 3.0 %collective-permute-start = (f32[16,1,128]{2,0,1:T(8,128)S(1)}, f32[16,1,128]{2,0,1:T(8,128)S(1)}, u32[]{:S(2)}, u32[]{:S(2)}) collective-permute-start(f32[16,1,128]{2,0,1:T(8,128)S(1)} %bitcast.112), channel_id=1, source_target_pairs={{0,4},{4,8},{8,12},{12,16},{16,20},{20,24},{24,28},{28,0},{1,5},{5... | collective-permute-start | bytes 24584 | tf_op jit(solution)/shard_map/ppermute | solution.py:16
  10.1 3.1 %collective-permute-start.1 = (f32[16,1,128]{2,0,1:T(8,128)S(1)}, f32[16,1,128]{2,0,1:T(8,128)S(1)}, u32[]{:S(2)}, u32[]{:S(2)}) collective-permute-start(f32[16,1,128]{2,0,1:T(8,128)S(1)} %bitcast.111), channel_id=1, source_target_pairs={{4,0},{8,4},{12,8},{16,12},{20,16},{24,20},{28,24},{0,28},{5,1},{9... | collective-permute-start | bytes 24584 | tf_op jit(solution)/shard_map/ppermute | solution.py:17
  13.3 0.7 copy-done.5
  14.8 5.4 %all_gather.9 = f32[2,64,128]{2,1,0:T(8,128)S(1)} all-gather(f32[2,16,128]{2,1,0:T(8,128)S(1)} %pad_maximum_fusion.6), channel_id=1, replica_groups=mesh['gx'=8,'gy'=4] {'gy'}, dimensions={1}, use_global_device_ids=true | all-gather | bytes 81920 | tf_op jit(solution)/shard_map/all_gather | solution.py:52
  22.2 0.7 multiply_reduce_fusion.14
  22.9 1.4 pad_maximum_fusion.9
  24.3 40.2 %psum.28 = f32[2]{0:T(128)S(1)} all-reduce(f32[2]{0:T(128)S(1)} %pad_maximum_fusion.9), channel_id=1, replica_groups=mesh['gx'=8,'gy'=4] {'gx','gy'}, use_global_device_ids=true, to_apply=%region_2.4 | all-reduce | flops 2 | bytes 16 | tf_op jit(solution)/shard_map/psum | solution.py:70
  66.8 2.3 collective-permute-start.4
  69.1 2.5 %collective-permute-start.5 = (f32[16,1,128]{2,0,1:T(8,128)S(1)}, f32[16,1,128]{2,0,1:T(8,128)S(1)}, u32[]{:S(2)}, u32[]{:S(2)}) collective-permute-start(f32[16,1,128]{2,0,1:T(8,128)S(1)} %bitcast.113), channel_id=1, source_target_pairs={{4,0},{8,4},{12,8},{16,12},{20,16},{24,20},{28,24},{0,28},{5,1},{9... | collective-permute-start | bytes 24584 | tf_op jit(solution)/shard_map/ppermute | solution.py:17
  71.6 1.3 collective-permute-start.6
  72.9 3.0 %collective-permute-start.7 = (f32[1,16,128]{2,1,0:T(8,128)S(1)}, f32[1,16,128]{2,1,0:T(8,128)S(1)}, u32[]{:S(2)}, u32[]{:S(2)}) collective-permute-start(f32[1,16,128]{2,1,0:T(8,128)S(1)} %get-tuple-element.42), channel_id=1, source_target_pairs={{0,1},{1,2},{2,3},{4,5},{5,6},{6,7},{8,9},{9,10},{10,11},{12,13},{... | collective-permute-start | bytes 24584 | tf_op jit(solution)/shard_map/ppermute | solution.py:16
  75.9 5.8 %all_gather.10 = f32[2,64,128]{2,1,0:T(8,128)S(1)} all-gather(f32[2,16,128]{2,1,0:T(8,128)S(1)} %pad_maximum_fusion.7), channel_id=1, replica_groups=mesh['gx'=8,'gy'=4] {'gy'}, dimensions={1}, use_global_device_ids=true | all-gather | bytes 81920 | tf_op jit(solution)/shard_map/all_gather | solution.py:52
  83.1 0.8 multiply_reduce_fusion.8
  83.8 3.2 %stack.76 = f32[5]{0:T(128)S(1)} concatenate(f32[1]{0:T(128)} %bitcast.28, f32[1]{0:T(128)} %bitcast.29, f32[1]{0:T(128)} %bitcast.30, f32[1]{0:T(128)} %bitcast.31, f32[1]{0:T(128)} %bitcast.32), dimensions={0} | concatenate | bytes 40 | tf_op jit(solution)/shard_map/stack | solution.py:70
  87.1 37.9 %psum.29 = f32[5]{0:T(128)S(1)} all-reduce(f32[5]{0:T(128)S(1)} %stack.76), channel_id=1, replica_groups=mesh['gx'=8,'gy'=4] {'gx','gy'}, use_global_device_ids=true, to_apply=%region_8.10 | all-reduce | flops 5 | bytes 40 | tf_op jit(solution)/shard_map/psum | solution.py:70
  130.4 2.3 collective-permute-start.8
  132.7 2.5 %collective-permute-start.9 = (f32[16,1,128]{2,0,1:T(8,128)S(1)}, f32[16,1,128]{2,0,1:T(8,128)S(1)}, u32[]{:S(2)}, u32[]{:S(2)}) collective-permute-start(f32[16,1,128]{2,0,1:T(8,128)S(1)} %bitcast.114), channel_id=1, source_target_pairs={{4,0},{8,4},{12,8},{16,12},{20,16},{24,20},{28,24},{0,28},{5,1},{9... | collective-permute-start | bytes 24584 | tf_op jit(solution)/shard_map/ppermute | solution.py:17
  135.2 1.3 collective-permute-start.10
  136.5 3.0 %collective-permute-start.11 = (f32[1,16,128]{2,1,0:T(8,128)S(1)}, f32[1,16,128]{2,1,0:T(8,128)S(1)}, u32[]{:S(2)}, u32[]{:S(2)}) collective-permute-start(f32[1,16,128]{2,1,0:T(8,128)S(1)} %get-tuple-element.36), channel_id=1, source_target_pairs={{0,1},{1,2},{2,3},{4,5},{5,6},{6,7},{8,9},{9,10},{10,11},{12,13},{... | collective-permute-start | bytes 24584 | tf_op jit(solution)/shard_map/ppermute | solution.py:16
  139.6 5.8 %all_gather.11 = f32[2,64,128]{2,1,0:T(8,128)S(1)} all-gather(f32[2,16,128]{2,1,0:T(8,128)S(1)} %pad_maximum_fusion.8), channel_id=1, replica_groups=mesh['gx'=8,'gy'=4] {'gy'}, dimensions={1}, use_global_device_ids=true | all-gather | bytes 81920 | tf_op jit(solution)/shard_map/all_gather | solution.py:52
  146.7 0.9 multiply_reduce_fusion.1
  147.5 4.5 %stack.85 = f32[7]{0:T(128)S(1)} concatenate(f32[1]{0:T(128)} %bitcast.46, f32[1]{0:T(128)} %bitcast.47, f32[1]{0:T(128)} %bitcast.48, f32[1]{0:T(128)} %bitcast.49, f32[1]{0:T(128)} %bitcast.50, f32[1]{0:T(128)} %bitcast.51, f32[1]{0:T(128)} %bitcast.52), dimensions={0} | concatenate | bytes 56 | tf_op jit(solution)/shard_map/stack | solution.py:70
  152.0 38.1 %psum.30 = f32[7]{0:T(128)S(1)} all-reduce(f32[7]{0:T(128)S(1)} %stack.85), channel_id=1, replica_groups=mesh['gx'=8,'gy'=4] {'gx','gy'}, use_global_device_ids=true, to_apply=%region_16.18 | all-reduce | flops 7 | bytes 56 | tf_op jit(solution)/shard_map/psum | solution.py:70
  190.1 0.8 multiply_reduce_fusion.16
  194.1 2.6 %multiply_add_fusion = f32[16,16,128]{2,1,0:T(8,128)} fusion(f32[16,16,128]{2,1,0:T(8,128)S(1)} %fusion.27, f32[16,16,128]{2,1,0:T(8,128)S(1)} %fusion.29, f32[16,16,128]{2,1,0:T(8,128)S(1)} %convolution_bitcast_fusion, f32[]{:T(128)S(6)} %sqrt.17, f32[]{:T(128)} %bitcast.56, f32[]{:T(128)} %bitcast.55, f32[]{:T(128)S(6)} %mul.267, f32[]{:T(128)} %bitcast.34, ...), kind=kLoop, calls=%fused_computation.51 | loop fusion | flops 458752 | bytes 524324 | tf_op jit(solution)/shard_map/add | solution.py:84
  196.7 2.5 %multiply_reduce_fusion = (f32[]{:T(128)}, f32[16,16,128]{2,1,0:T(8,128)}) fusion(f32[16,16,128]{2,1,0:T(8,128)S(1)} %get-tuple-element.23, f32[]{:T(128)S(6)} %sqrt.17, f32[16,16,128]{2,1,0:T(8,128)S(1)} %get-tuple-element.24, f32[]{:T(128)} %bitcast.56, f32[16,16,128]{2,1,0:T(8,128)S(1)} %get-tuple-element.22, f32[16,16,128]{2,1,0:T(8,128)S(1)} %get-tuple-element.26, ...), kind=kLoop, calls=%fused_computation.49 | loop fusion | flops 327679 | bytes 655384 | tf_op jit(solution)/shard_map/reduce_sum | solution.py:23
  199.2 41.3 %psum.31 = f32[]{:T(128)} all-reduce(f32[]{:T(128)} %get-tuple-element.20), channel_id=1, replica_groups=mesh['gx'=8,'gy'=4] {'gx','gy'}, use_global_device_ids=true, to_apply=%region_20.22 | all-reduce | flops 1 | bytes 8 | tf_op jit(solution)/shard_map/psum | solution.py:88
  241.2 1.8 pad_maximum_fusion.10
  (64 shorter events, 8.5 us)
Async XLA Ops:
  0.6 0.9 copy-start
  2.7 18.8 %collective-permute-start.2 = (f32[1,16,128]{2,1,0:T(8,128)S(1)}, f32[1,16,128]{2,1,0:T(8,128)S(1)}, u32[]{:S(2)}, u32[]{:S(2)}) collective-permute-start(f32[1,16,128]{2,1,0:T(8,128)S(1)} %get-tuple-element.47), channel_id=1, source_target_pairs={{1,0},{2,1},{3,2},{5,4},{6,5},{7,6},{9,8},{10,9},{11,10},{13,12},{... | collective-permute-start | bytes 24584 | tf_op jit(solution)/shard_map/ppermute | solution.py:17
  4.0 17.5 %collective-permute-start.3 = (f32[1,16,128]{2,1,0:T(8,128)S(1)}, f32[1,16,128]{2,1,0:T(8,128)S(1)}, u32[]{:S(2)}, u32[]{:S(2)}) collective-permute-start(f32[1,16,128]{2,1,0:T(8,128)S(1)} %get-tuple-element.48), channel_id=1, source_target_pairs={{0,1},{1,2},{2,3},{4,5},{5,6},{6,7},{8,9},{9,10},{10,11},{12,13},{... | collective-permute-start | bytes 24584 | tf_op jit(solution)/shard_map/ppermute | solution.py:16
  7.1 7.7 %collective-permute-start = (f32[16,1,128]{2,0,1:T(8,128)S(1)}, f32[16,1,128]{2,0,1:T(8,128)S(1)}, u32[]{:S(2)}, u32[]{:S(2)}) collective-permute-start(f32[16,1,128]{2,0,1:T(8,128)S(1)} %bitcast.112), channel_id=1, source_target_pairs={{0,4},{4,8},{8,12},{12,16},{16,20},{20,24},{24,28},{28,0},{1,5},{5... | collective-permute-start | bytes 24584 | tf_op jit(solution)/shard_map/ppermute | solution.py:16
  10.1 4.7 %collective-permute-start.1 = (f32[16,1,128]{2,0,1:T(8,128)S(1)}, f32[16,1,128]{2,0,1:T(8,128)S(1)}, u32[]{:S(2)}, u32[]{:S(2)}) collective-permute-start(f32[16,1,128]{2,0,1:T(8,128)S(1)} %bitcast.111), channel_id=1, source_target_pairs={{4,0},{8,4},{12,8},{16,12},{20,16},{24,20},{28,24},{0,28},{5,1},{9... | collective-permute-start | bytes 24584 | tf_op jit(solution)/shard_map/ppermute | solution.py:17
  13.3 0.7 copy-start.5
  14.8 6.7 %copy-start.3 = (f32[16,16,128]{2,1,0:T(8,128)S(1)}, f32[16,16,128]{2,1,0:T(8,128)}, u32[]{:S(2)}) copy-start(f32[16,16,128]{2,1,0:T(8,128)} %param.9) | copy-start | bytes 393220
  20.2 1.3 copy-start.2
  20.2 1.3 copy-start.1
  21.5 0.7 copy-start.4
  66.8 9.1 %collective-permute-start.4 = (f32[16,1,128]{2,0,1:T(8,128)S(1)}, f32[16,1,128]{2,0,1:T(8,128)S(1)}, u32[]{:S(2)}, u32[]{:S(2)}) collective-permute-start(f32[16,1,128]{2,0,1:T(8,128)S(1)} %bitcast.115), channel_id=1, source_target_pairs={{0,4},{4,8},{8,12},{12,16},{16,20},{20,24},{24,28},{28,0},{1,5},{5... | collective-permute-start | bytes 24584 | tf_op jit(solution)/shard_map/ppermute | solution.py:16
  69.1 6.8 %collective-permute-start.5 = (f32[16,1,128]{2,0,1:T(8,128)S(1)}, f32[16,1,128]{2,0,1:T(8,128)S(1)}, u32[]{:S(2)}, u32[]{:S(2)}) collective-permute-start(f32[16,1,128]{2,0,1:T(8,128)S(1)} %bitcast.113), channel_id=1, source_target_pairs={{4,0},{8,4},{12,8},{16,12},{20,16},{24,20},{28,24},{0,28},{5,1},{9... | collective-permute-start | bytes 24584 | tf_op jit(solution)/shard_map/ppermute | solution.py:17
  71.6 11.5 %collective-permute-start.6 = (f32[1,16,128]{2,1,0:T(8,128)S(1)}, f32[1,16,128]{2,1,0:T(8,128)S(1)}, u32[]{:S(2)}, u32[]{:S(2)}) collective-permute-start(f32[1,16,128]{2,1,0:T(8,128)S(1)} %get-tuple-element.41), channel_id=1, source_target_pairs={{1,0},{2,1},{3,2},{5,4},{6,5},{7,6},{9,8},{10,9},{11,10},{13,12},{... | collective-permute-start | bytes 24584 | tf_op jit(solution)/shard_map/ppermute | solution.py:17
  72.9 10.2 %collective-permute-start.7 = (f32[1,16,128]{2,1,0:T(8,128)S(1)}, f32[1,16,128]{2,1,0:T(8,128)S(1)}, u32[]{:S(2)}, u32[]{:S(2)}) collective-permute-start(f32[1,16,128]{2,1,0:T(8,128)S(1)} %get-tuple-element.42), channel_id=1, source_target_pairs={{0,1},{1,2},{2,3},{4,5},{5,6},{6,7},{8,9},{9,10},{10,11},{12,13},{... | collective-permute-start | bytes 24584 | tf_op jit(solution)/shard_map/ppermute | solution.py:16
  130.4 9.1 %collective-permute-start.8 = (f32[16,1,128]{2,0,1:T(8,128)S(1)}, f32[16,1,128]{2,0,1:T(8,128)S(1)}, u32[]{:S(2)}, u32[]{:S(2)}) collective-permute-start(f32[16,1,128]{2,0,1:T(8,128)S(1)} %bitcast.116), channel_id=1, source_target_pairs={{0,4},{4,8},{8,12},{12,16},{16,20},{20,24},{24,28},{28,0},{1,5},{5... | collective-permute-start | bytes 24584 | tf_op jit(solution)/shard_map/ppermute | solution.py:16
  132.7 6.8 %collective-permute-start.9 = (f32[16,1,128]{2,0,1:T(8,128)S(1)}, f32[16,1,128]{2,0,1:T(8,128)S(1)}, u32[]{:S(2)}, u32[]{:S(2)}) collective-permute-start(f32[16,1,128]{2,0,1:T(8,128)S(1)} %bitcast.114), channel_id=1, source_target_pairs={{4,0},{8,4},{12,8},{16,12},{20,16},{24,20},{28,24},{0,28},{5,1},{9... | collective-permute-start | bytes 24584 | tf_op jit(solution)/shard_map/ppermute | solution.py:17
  135.2 11.5 %collective-permute-start.10 = (f32[1,16,128]{2,1,0:T(8,128)S(1)}, f32[1,16,128]{2,1,0:T(8,128)S(1)}, u32[]{:S(2)}, u32[]{:S(2)}) collective-permute-start(f32[1,16,128]{2,1,0:T(8,128)S(1)} %get-tuple-element.35), channel_id=1, source_target_pairs={{1,0},{2,1},{3,2},{5,4},{6,5},{7,6},{9,8},{10,9},{11,10},{13,12},{... | collective-permute-start | bytes 24584 | tf_op jit(solution)/shard_map/ppermute | solution.py:17
  136.5 10.2 %collective-permute-start.11 = (f32[1,16,128]{2,1,0:T(8,128)S(1)}, f32[1,16,128]{2,1,0:T(8,128)S(1)}, u32[]{:S(2)}, u32[]{:S(2)}) collective-permute-start(f32[1,16,128]{2,1,0:T(8,128)S(1)} %get-tuple-element.36), channel_id=1, source_target_pairs={{0,1},{1,2},{2,3},{4,5},{5,6},{6,7},{8,9},{9,10},{10,11},{12,13},{... | collective-permute-start | bytes 24584 | tf_op jit(solution)/shard_map/ppermute | solution.py:16
where the time goes:
time: 244 us; the launch traced here: 243 us
  blocking collectives  175 us (72%)
  starting transfers between devices  28.6 us (12%)
  local copies, waits for them, and re-layouts  15.2 us (6%)
  other arithmetic  12.7 us (5%)
  between operations  9.45 us (4%)
    psum x3, blocking collectives, on_device(): totals = lax.psum(jnp.stack(terms), ('gx', 'gy')) / total_cells  116 us
    psum x1, blocking collectives, on_device(): lax.psum(local_product(residual, residual), ('gx', 'gy')) / total_cells  41.3 us
    all_gather x3, blocking collectives, on_device(): whole = lax.all_gather(edges, 'gy', axis=1, tiled=True)  17 us
    ppermute x6, starting transfers between devices, padded(): before = lax.ppermute(last, axis, up)  16.8 us
    ppermute x6, starting transfers between devices, padded(): after = lax.ppermute(initial, axis, down)  11.9 us
    another operation x2, local copies, waits for them, and re-layouts, on_device(): totals = lax.psum(jnp.stack(terms), ('gx', 'gy')) / total_cells  7.69 us
    reduce_sum x4, other arithmetic, local_product(): return jnp.sum(left * right)  4.94 us
  transfers between devices with their start and end apart: 12, of which 1 were waited for; matrix products, arithmetic and copies ran while one was open for 2% of the time, Pallas kernels for 0%

commit v1 on v0

--- a/solution.py
+++ b/solution.py
@@ -67,7 +67,7 @@
         terms = terms + [local_product(image, image), local_product(residual, image)]
         if step > 0:
             terms.append(local_product(residual, residual))
-        totals = lax.psum(jnp.stack(terms), ("gx", "gy")) / total_cells
+        totals = lax.psum(lax.psum(jnp.stack(terms), "gy"), "gx") / total_cells
         coeffs = totals[:count]
         against = totals[count : 2 * count]
         square = totals[2 * count] - jnp.sum(coeffs * coeffs)

time: 244 us -> 203 us (0.83)
  blocking collectives: 175 us -> 133 us
    psum x3 -> x6, blocking collectives: 116 us -> 80.4 us  [on_device(): totals = lax.psum(lax.psum(jnp.stack(terms), 'gy'), 'gx') / total_cells]
    ppermute x6, starting transfers between devices: 16.8 us -> 12.3 us  [padded(): before = lax.ppermute(last, axis, up)]
    ppermute x6, starting transfers between devices: 11.9 us -> 16.3 us  [padded(): after = lax.ppermute(initial, axis, down)]
    psum x1, blocking collectives: 41.3 us -> 37 us  [on_device(): lax.psum(local_product(residual, residual), ('gx', 'gy')) / total_cells]
where the time goes in v1:
time: 203 us; the launch traced here: 202 us
  blocking collectives  133 us (66%)
  starting transfers between devices  28.6 us (14%)
  local copies, waits for them, and re-layouts  15.2 us (7%)
  other arithmetic  12.7 us (6%)
  between operations  9.46 us (5%)
    psum x6, blocking collectives, on_device(): totals = lax.psum(lax.psum(jnp.stack(terms), 'gy'), 'gx') / total_cells  80.4 us
    psum x1, blocking collectives, on_device(): lax.psum(local_product(residual, residual), ('gx', 'gy')) / total_cells  37 us
    ppermute x6, starting transfers between devices, padded(): after = lax.ppermute(initial, axis, down)  16.3 us
    all_gather x3, blocking collectives, on_device(): whole = lax.all_gather(edges, 'gy', axis=1, tiled=True)  15.8 us
    ppermute x6, starting transfers between devices, padded(): before = lax.ppermute(last, axis, up)  12.3 us
    another operation x2, local copies, waits for them, and re-layouts, on_device(): totals = lax.psum(lax.psum(jnp.stack(terms), 'gy'), 'gx') / total_cells  7.69 us
    reduce_sum x4, other arithmetic, local_product(): return jnp.sum(left * right)  4.94 us
  transfers between devices with their start and end apart: 12, of which 1 were waited for; matrix products, arithmetic and copies ran while one was open for 2% of the time, Pallas kernels for 0%

profile of v1, /device:TPU:0, one launch (start us, length us, event | category | flops | bytes accessed | tf_op | source)
XLA Modules:
  0.0 201.7 jit_solution(12590225492900633149)
XLA Ops:
  0.7 0.9 copy-done
  1.5 1.2 convolution_bitcast_fusion
  2.7 1.3 collective-permute-start.2
  4.0 3.0 %collective-permute-start.3 = (f32[1,16,128]{2,1,0:T(8,128)S(1)}, f32[1,16,128]{2,1,0:T(8,128)S(1)}, u32[]{:S(2)}, u32[]{:S(2)}) collective-permute-start(f32[1,16,128]{2,1,0:T(8,128)S(1)} %get-tuple-element.48), channel_id=1, source_target_pairs={{0,1},{1,2},{2,3},{4,5},{5,6},{6,7},{8,9},{9,10},{10,11},{12,13},{... | collective-permute-start | bytes 24584 | tf_op jit(solution)/shard_map/ppermute | solution.py:16
  7.1 3.0 %collective-permute-start = (f32[16,1,128]{2,0,1:T(8,128)S(1)}, f32[16,1,128]{2,0,1:T(8,128)S(1)}, u32[]{:S(2)}, u32[]{:S(2)}) collective-permute-start(f32[16,1,128]{2,0,1:T(8,128)S(1)} %bitcast.112), channel_id=1, source_target_pairs={{0,4},{4,8},{8,12},{12,16},{16,20},{20,24},{24,28},{28,0},{1,5},{5... | collective-permute-start | bytes 24584 | tf_op jit(solution)/shard_map/ppermute | solution.py:16
  10.1 3.1 %collective-permute-start.1 = (f32[16,1,128]{2,0,1:T(8,128)S(1)}, f32[16,1,128]{2,0,1:T(8,128)S(1)}, u32[]{:S(2)}, u32[]{:S(2)}) collective-permute-start(f32[16,1,128]{2,0,1:T(8,128)S(1)} %bitcast.111), channel_id=1, source_target_pairs={{4,0},{8,4},{12,8},{16,12},{20,16},{24,20},{28,24},{0,28},{5,1},{9... | collective-permute-start | bytes 24584 | tf_op jit(solution)/shard_map/ppermute | solution.py:17
  14.8 5.4 %all_gather.9 = f32[2,64,128]{2,1,0:T(8,128)S(1)} all-gather(f32[2,16,128]{2,1,0:T(8,128)S(1)} %pad_maximum_fusion.6), channel_id=1, replica_groups=mesh['gx'=8,'gy'=4] {'gy'}, dimensions={1}, use_global_device_ids=true | all-gather | bytes 81920 | tf_op jit(solution)/shard_map/all_gather | solution.py:52
  22.2 0.7 multiply_reduce_fusion.14
  22.9 1.4 pad_maximum_fusion.9
  24.3 7.2 %psum.49 = f32[2]{0:T(128)S(1)} all-reduce(f32[2]{0:T(128)S(1)} %pad_maximum_fusion.9), channel_id=1, replica_groups=mesh['gx'=8,'gy'=4] {'gy'}, use_global_device_ids=true, to_apply=%region_2.4 | all-reduce | flops 2 | bytes 16 | tf_op jit(solution)/shard_map/psum | solution.py:70
  31.5 21.8 %psum.50 = f32[2]{0:T(128)S(1)} all-reduce(f32[2]{0:T(128)S(1)} %psum.49), channel_id=1, replica_groups=mesh['gx'=8,'gy'=4] {'gx'}, use_global_device_ids=true, to_apply=%region_3.5 | all-reduce | flops 2 | bytes 16 | tf_op jit(solution)/shard_map/psum | solution.py:70
  55.7 4.7 %collective-permute-start.5 = (f32[16,1,128]{2,0,1:T(8,128)S(1)}, f32[16,1,128]{2,0,1:T(8,128)S(1)}, u32[]{:S(2)}, u32[]{:S(2)}) collective-permute-start(f32[16,1,128]{2,0,1:T(8,128)S(1)} %bitcast.113), channel_id=1, source_target_pairs={{4,0},{8,4},{12,8},{16,12},{20,16},{24,20},{28,24},{0,28},{5,1},{9... | collective-permute-start | bytes 24584 | tf_op jit(solution)/shard_map/ppermute | solution.py:17
  60.4 1.3 collective-permute-start.6
  61.7 3.0 %collective-permute-start.7 = (f32[1,16,128]{2,1,0:T(8,128)S(1)}, f32[1,16,128]{2,1,0:T(8,128)S(1)}, u32[]{:S(2)}, u32[]{:S(2)}) collective-permute-start(f32[1,16,128]{2,1,0:T(8,128)S(1)} %get-tuple-element.42), channel_id=1, source_target_pairs={{0,1},{1,2},{2,3},{4,5},{5,6},{6,7},{8,9},{9,10},{10,11},{12,13},{... | collective-permute-start | bytes 24584 | tf_op jit(solution)/shard_map/ppermute | solution.py:16
  64.7 5.2 %all_gather.10 = f32[2,64,128]{2,1,0:T(8,128)S(1)} all-gather(f32[2,16,128]{2,1,0:T(8,128)S(1)} %pad_maximum_fusion.7), channel_id=1, replica_groups=mesh['gx'=8,'gy'=4] {'gy'}, dimensions={1}, use_global_device_ids=true | all-gather | bytes 81920 | tf_op jit(solution)/shard_map/all_gather | solution.py:52
  71.3 0.8 multiply_reduce_fusion.8
  72.1 3.2 %stack.76 = f32[5]{0:T(128)S(1)} concatenate(f32[1]{0:T(128)} %bitcast.28, f32[1]{0:T(128)} %bitcast.29, f32[1]{0:T(128)} %bitcast.30, f32[1]{0:T(128)} %bitcast.31, f32[1]{0:T(128)} %bitcast.32), dimensions={0} | concatenate | bytes 40 | tf_op jit(solution)/shard_map/stack | solution.py:70
  75.3 6.0 %psum.51 = f32[5]{0:T(128)S(1)} all-reduce(f32[5]{0:T(128)S(1)} %stack.76), channel_id=1, replica_groups=mesh['gx'=8,'gy'=4] {'gy'}, use_global_device_ids=true, to_apply=%region_9.11 | all-reduce | flops 5 | bytes 40 | tf_op jit(solution)/shard_map/psum | solution.py:70
  81.3 19.1 %psum.52 = f32[5]{0:T(128)S(1)} all-reduce(f32[5]{0:T(128)S(1)} %psum.51), channel_id=1, replica_groups=mesh['gx'=8,'gy'=4] {'gx'}, use_global_device_ids=true, to_apply=%region_10.12 | all-reduce | flops 5 | bytes 40 | tf_op jit(solution)/shard_map/psum | solution.py:70
  106.0 4.7 %collective-permute-start.9 = (f32[16,1,128]{2,0,1:T(8,128)S(1)}, f32[16,1,128]{2,0,1:T(8,128)S(1)}, u32[]{:S(2)}, u32[]{:S(2)}) collective-permute-start(f32[16,1,128]{2,0,1:T(8,128)S(1)} %bitcast.114), channel_id=1, source_target_pairs={{4,0},{8,4},{12,8},{16,12},{20,16},{24,20},{28,24},{0,28},{5,1},{9... | collective-permute-start | bytes 24584 | tf_op jit(solution)/shard_map/ppermute | solution.py:17
  110.6 1.3 collective-permute-start.10
  111.9 3.0 %collective-permute-start.11 = (f32[1,16,128]{2,1,0:T(8,128)S(1)}, f32[1,16,128]{2,1,0:T(8,128)S(1)}, u32[]{:S(2)}, u32[]{:S(2)}) collective-permute-start(f32[1,16,128]{2,1,0:T(8,128)S(1)} %get-tuple-element.36), channel_id=1, source_target_pairs={{0,1},{1,2},{2,3},{4,5},{5,6},{6,7},{8,9},{9,10},{10,11},{12,13},{... | collective-permute-start | bytes 24584 | tf_op jit(solution)/shard_map/ppermute | solution.py:16
  115.0 5.2 %all_gather.11 = f32[2,64,128]{2,1,0:T(8,128)S(1)} all-gather(f32[2,16,128]{2,1,0:T(8,128)S(1)} %pad_maximum_fusion.8), channel_id=1, replica_groups=mesh['gx'=8,'gy'=4] {'gy'}, dimensions={1}, use_global_device_ids=true | all-gather | bytes 81920 | tf_op jit(solution)/shard_map/all_gather | solution.py:52
  121.5 0.9 multiply_reduce_fusion.1
  122.4 4.5 %stack.85 = f32[7]{0:T(128)S(1)} concatenate(f32[1]{0:T(128)} %bitcast.46, f32[1]{0:T(128)} %bitcast.47, f32[1]{0:T(128)} %bitcast.48, f32[1]{0:T(128)} %bitcast.49, f32[1]{0:T(128)} %bitcast.50, f32[1]{0:T(128)} %bitcast.51, f32[1]{0:T(128)} %bitcast.52), dimensions={0} | concatenate | bytes 56 | tf_op jit(solution)/shard_map/stack | solution.py:70
  126.9 7.2 %psum.53 = f32[7]{0:T(128)S(1)} all-reduce(f32[7]{0:T(128)S(1)} %stack.85), channel_id=1, replica_groups=mesh['gx'=8,'gy'=4] {'gy'}, use_global_device_ids=true, to_apply=%region_18.20 | all-reduce | flops 7 | bytes 56 | tf_op jit(solution)/shard_map/psum | solution.py:70
  134.1 19.1 %psum.54 = f32[7]{0:T(128)S(1)} all-reduce(f32[7]{0:T(128)S(1)} %psum.53), channel_id=1, replica_groups=mesh['gx'=8,'gy'=4] {'gx'}, use_global_device_ids=true, to_apply=%region_19.21 | all-reduce | flops 7 | bytes 56 | tf_op jit(solution)/shard_map/psum | solution.py:70
  153.2 0.8 multiply_reduce_fusion.16
  157.2 2.6 %multiply_add_fusion = f32[16,16,128]{2,1,0:T(8,128)} fusion(f32[16,16,128]{2,1,0:T(8,128)S(1)} %fusion.27, f32[16,16,128]{2,1,0:T(8,128)S(1)} %fusion.29, f32[16,16,128]{2,1,0:T(8,128)S(1)} %convolution_bitcast_fusion, f32[]{:T(128)S(6)} %sqrt.17, f32[]{:T(128)} %bitcast.56, f32[]{:T(128)} %bitcast.55, f32[]{:T(128)S(6)} %mul.267, f32[]{:T(128)} %bitcast.34, ...), kind=kLoop, calls=%fused_computation.51 | loop fusion | flops 458752 | bytes 524324 | tf_op jit(solution)/shard_map/add | solution.py:84
  159.8 2.5 %multiply_reduce_fusion = (f32[]{:T(128)}, f32[16,16,128]{2,1,0:T(8,128)}) fusion(f32[16,16,128]{2,1,0:T(8,128)S(1)} %get-tuple-element.23, f32[]{:T(128)S(6)} %sqrt.17, f32[16,16,128]{2,1,0:T(8,128)S(1)} %get-tuple-element.24, f32[]{:T(128)} %bitcast.56, f32[16,16,128]{2,1,0:T(8,128)S(1)} %get-tuple-element.22, f32[16,16,128]{2,1,0:T(8,128)S(1)} %get-tuple-element.26, ...), kind=kLoop, calls=%fused_computation.49 | loop fusion | flops 327679 | bytes 655384 | tf_op jit(solution)/shard_map/reduce_sum | solution.py:23
  162.3 37.0 %psum.55 = f32[]{:T(128)} all-reduce(f32[]{:T(128)} %get-tuple-element.20), channel_id=1, replica_groups=mesh['gx'=8,'gy'=4] {'gx','gy'}, use_global_device_ids=true, to_apply=%region_23.25 | all-reduce | flops 1 | bytes 8 | tf_op jit(solution)/shard_map/psum | solution.py:88
  200.0 1.8 pad_maximum_fusion.10
  (67 shorter events, 9.4 us)
Async XLA Ops:
  0.6 0.9 copy-start
  2.7 18.8 %collective-permute-start.2 = (f32[1,16,128]{2,1,0:T(8,128)S(1)}, f32[1,16,128]{2,1,0:T(8,128)S(1)}, u32[]{:S(2)}, u32[]{:S(2)}) collective-permute-start(f32[1,16,128]{2,1,0:T(8,128)S(1)} %get-tuple-element.47), channel_id=1, source_target_pairs={{1,0},{2,1},{3,2},{5,4},{6,5},{7,6},{9,8},{10,9},{11,10},{13,12},{... | collective-permute-start | bytes 24584 | tf_op jit(solution)/shard_map/ppermute | solution.py:17
  4.0 17.5 %collective-permute-start.3 = (f32[1,16,128]{2,1,0:T(8,128)S(1)}, f32[1,16,128]{2,1,0:T(8,128)S(1)}, u32[]{:S(2)}, u32[]{:S(2)}) collective-permute-start(f32[1,16,128]{2,1,0:T(8,128)S(1)} %get-tuple-element.48), channel_id=1, source_target_pairs={{0,1},{1,2},{2,3},{4,5},{5,6},{6,7},{8,9},{9,10},{10,11},{12,13},{... | collective-permute-start | bytes 24584 | tf_op jit(solution)/shard_map/ppermute | solution.py:16
  7.1 7.7 %collective-permute-start = (f32[16,1,128]{2,0,1:T(8,128)S(1)}, f32[16,1,128]{2,0,1:T(8,128)S(1)}, u32[]{:S(2)}, u32[]{:S(2)}) collective-permute-start(f32[16,1,128]{2,0,1:T(8,128)S(1)} %bitcast.112), channel_id=1, source_target_pairs={{0,4},{4,8},{8,12},{12,16},{16,20},{20,24},{24,28},{28,0},{1,5},{5... | collective-permute-start | bytes 24584 | tf_op jit(solution)/shard_map/ppermute | solution.py:16
  10.1 4.7 %collective-permute-start.1 = (f32[16,1,128]{2,0,1:T(8,128)S(1)}, f32[16,1,128]{2,0,1:T(8,128)S(1)}, u32[]{:S(2)}, u32[]{:S(2)}) collective-permute-start(f32[16,1,128]{2,0,1:T(8,128)S(1)} %bitcast.111), channel_id=1, source_target_pairs={{4,0},{8,4},{12,8},{16,12},{20,16},{24,20},{28,24},{0,28},{5,1},{9... | collective-permute-start | bytes 24584 | tf_op jit(solution)/shard_map/ppermute | solution.py:17
  13.3 0.7 copy-start.5
  14.8 6.7 %copy-start.3 = (f32[16,16,128]{2,1,0:T(8,128)S(1)}, f32[16,16,128]{2,1,0:T(8,128)}, u32[]{:S(2)}) copy-start(f32[16,16,128]{2,1,0:T(8,128)} %param.9) | copy-start | bytes 393220
  20.2 1.3 copy-start.2
  20.2 1.3 copy-start.1
  21.5 0.7 copy-start.4
  55.6 9.1 %collective-permute-start.4 = (f32[16,1,128]{2,0,1:T(8,128)S(1)}, f32[16,1,128]{2,0,1:T(8,128)S(1)}, u32[]{:S(2)}, u32[]{:S(2)}) collective-permute-start(f32[16,1,128]{2,0,1:T(8,128)S(1)} %bitcast.115), channel_id=1, source_target_pairs={{0,4},{4,8},{8,12},{12,16},{16,20},{20,24},{24,28},{28,0},{1,5},{5... | collective-permute-start | bytes 24584 | tf_op jit(solution)/shard_map/ppermute | solution.py:16
  55.7 9.1 %collective-permute-start.5 = (f32[16,1,128]{2,0,1:T(8,128)S(1)}, f32[16,1,128]{2,0,1:T(8,128)S(1)}, u32[]{:S(2)}, u32[]{:S(2)}) collective-permute-start(f32[16,1,128]{2,0,1:T(8,128)S(1)} %bitcast.113), channel_id=1, source_target_pairs={{4,0},{8,4},{12,8},{16,12},{20,16},{24,20},{28,24},{0,28},{5,1},{9... | collective-permute-start | bytes 24584 | tf_op jit(solution)/shard_map/ppermute | solution.py:17
  60.4 10.9 %collective-permute-start.6 = (f32[1,16,128]{2,1,0:T(8,128)S(1)}, f32[1,16,128]{2,1,0:T(8,128)S(1)}, u32[]{:S(2)}, u32[]{:S(2)}) collective-permute-start(f32[1,16,128]{2,1,0:T(8,128)S(1)} %get-tuple-element.41), channel_id=1, source_target_pairs={{1,0},{2,1},{3,2},{5,4},{6,5},{7,6},{9,8},{10,9},{11,10},{13,12},{... | collective-permute-start | bytes 24584 | tf_op jit(solution)/shard_map/ppermute | solution.py:17
  61.7 9.6 %collective-permute-start.7 = (f32[1,16,128]{2,1,0:T(8,128)S(1)}, f32[1,16,128]{2,1,0:T(8,128)S(1)}, u32[]{:S(2)}, u32[]{:S(2)}) collective-permute-start(f32[1,16,128]{2,1,0:T(8,128)S(1)} %get-tuple-element.42), channel_id=1, source_target_pairs={{0,1},{1,2},{2,3},{4,5},{5,6},{6,7},{8,9},{9,10},{10,11},{12,13},{... | collective-permute-start | bytes 24584 | tf_op jit(solution)/shard_map/ppermute | solution.py:16
  105.9 9.1 %collective-permute-start.8 = (f32[16,1,128]{2,0,1:T(8,128)S(1)}, f32[16,1,128]{2,0,1:T(8,128)S(1)}, u32[]{:S(2)}, u32[]{:S(2)}) collective-permute-start(f32[16,1,128]{2,0,1:T(8,128)S(1)} %bitcast.116), channel_id=1, source_target_pairs={{0,4},{4,8},{8,12},{12,16},{16,20},{20,24},{24,28},{28,0},{1,5},{5... | collective-permute-start | bytes 24584 | tf_op jit(solution)/shard_map/ppermute | solution.py:16
  106.0 9.0 %collective-permute-start.9 = (f32[16,1,128]{2,0,1:T(8,128)S(1)}, f32[16,1,128]{2,0,1:T(8,128)S(1)}, u32[]{:S(2)}, u32[]{:S(2)}) collective-permute-start(f32[16,1,128]{2,0,1:T(8,128)S(1)} %bitcast.114), channel_id=1, source_target_pairs={{4,0},{8,4},{12,8},{16,12},{20,16},{24,20},{28,24},{0,28},{5,1},{9... | collective-permute-start | bytes 24584 | tf_op jit(solution)/shard_map/ppermute | solution.py:17
  110.6 10.9 %collective-permute-start.10 = (f32[1,16,128]{2,1,0:T(8,128)S(1)}, f32[1,16,128]{2,1,0:T(8,128)S(1)}, u32[]{:S(2)}, u32[]{:S(2)}) collective-permute-start(f32[1,16,128]{2,1,0:T(8,128)S(1)} %get-tuple-element.35), channel_id=1, source_target_pairs={{1,0},{2,1},{3,2},{5,4},{6,5},{7,6},{9,8},{10,9},{11,10},{13,12},{... | collective-permute-start | bytes 24584 | tf_op jit(solution)/shard_map/ppermute | solution.py:17
  111.9 9.6 %collective-permute-start.11 = (f32[1,16,128]{2,1,0:T(8,128)S(1)}, f32[1,16,128]{2,1,0:T(8,128)S(1)}, u32[]{:S(2)}, u32[]{:S(2)}) collective-permute-start(f32[1,16,128]{2,1,0:T(8,128)S(1)} %get-tuple-element.36), channel_id=1, source_target_pairs={{0,1},{1,2},{2,3},{4,5},{5,6},{6,7},{8,9},{9,10},{10,11},{12,13},{... | collective-permute-start | bytes 24584 | tf_op jit(solution)/shard_map/ppermute | solution.py:16
